TPU v7x, 32 devices: a whole 2x2x4 slice. The times are simulated.
32 devices in a mesh: groups: 2 (over y), snap: 4 (over x, core), space: 4 (over z).
Axes of the slice: x: 2, y: 2, z: 4, core: 2. Of those that a mesh axis runs over, the one named last changes fastest.
Arguments:
- snapshots: bfloat16 [16384, 4096], P('space', ('groups', 'snap')), parts along dimension 1, may hold values from -12 to 12
- factor_blocks: bfloat16 [128, 4, 128, 128], P('space'), may hold values from -0.375 to 0.375
- factor_cols: int32 [128, 4], P('space'), may hold values from 0 to 31, as said below
- factor_counts: int32 [128], P('space'), may hold values from 1 to 4, as said below
- start_basis: float32 [4096, 128], P(('groups', 'snap')), parts along dimension 0, may hold values from -150 to 150
- merge_starts: float32 [3, 256, 128], replicated, may hold values from -150 to 150
Outputs:
- modes: bfloat16 [16384, 256], P(('space', 'snap'), 'groups'), parts along dimension 1
There are 2 independent parts, one for each index of `groups`. A program takes and returns all parts, laid end to end along the dimension named above; an argument that names none is the same for every part. Nothing has to cross between parts.
Inputs may be any that keep to these rules, and one draw needn't show every extreme that they name: `factor_cols`: each entry names one of the 32 row blocks of the same group as its row block. `factor_counts`: slots at or after the count are not part of the factor.
All inputs are finite; a program needn't handle non-finite values.
Results may differ from a plain program's by a relative error of at most 0.011.
Values may be sent and summed in bfloat16 or wider, within the bound.
A program may use at most 128 MiB of HBM per device.

v0:
```python
import jax
import jax.numpy as jnp
from jax import lax
from jax.sharding import PartitionSpec as P

HIGH = lax.Precision.HIGHEST


def from_partner(block, axis, bit):
    count = lax.axis_size(axis)
    route = []
    for low in range(count):
        high = low | 1 << bit
        if high != low and high < count:
            route += [(low, high), (high, low)]
    return lax.ppermute(block, axis, route)


def orthonormal(matrix):
    cross_gram = jnp.dot(matrix.T, matrix, precision=HIGH)
    lower_factor = jnp.linalg.cholesky(cross_gram)
    return lax.linalg.triangular_solve(
        lower_factor, matrix, left_side=False, lower=True, transpose_a=True
    )


def weigh(snapshots, factor_blocks, factor_cols, factor_counts):
    row_blocks, slot_count = factor_cols.shape
    block_width = factor_blocks.shape[2]
    column_count = snapshots.shape[1]
    blocks_in = snapshots.reshape(row_blocks, block_width, column_count)
    accumulated = jnp.zeros((row_blocks, block_width, column_count), jnp.float32)
    for slot_index in range(slot_count):
        live_mask = (slot_index < factor_counts)[:, None, None]
        factor = jnp.where(live_mask, factor_blocks[:, slot_index], jnp.zeros((), jnp.bfloat16))
        source = jnp.take(blocks_in, factor_cols[:, slot_index], axis=0)
        accumulated = accumulated + jnp.einsum(
            "bij,bjs->bis", factor, source, preferred_element_type=jnp.float32
        )
    return accumulated.astype(jnp.bfloat16).reshape(row_blocks * block_width, column_count)


def merge_level(paired, start_vectors, summed):
    local_cross = jnp.einsum("prk,prl->pkl", paired, paired, preferred_element_type=jnp.float32)
    cross_gram = summed(local_cross)
    steered = jnp.einsum("pkl,plm->pkm", cross_gram, start_vectors, precision=HIGH)
    mixing = jax.vmap(orthonormal)(steered).astype(jnp.bfloat16)
    return jnp.einsum("prk,pkm->prm", paired, mixing, preferred_element_type=jnp.float32).astype(
        jnp.bfloat16
    )


def local(snapshots, factor_blocks, factor_cols, factor_counts, start_basis, merge_starts):
    weighted = weigh(snapshots, factor_blocks, factor_cols, factor_counts)
    basis = start_basis
    own_gram = lax.psum_scatter(
        lax.dot_general(
            weighted, weighted, (((0,), (0,)), ((), ())), preferred_element_type=jnp.float32
        ),
        "space",
        scatter_dimension=0,
        tiled=True,
    )
    for sweep_index in range(2):
        own_rows = jnp.dot(own_gram, basis, precision=HIGH)
        cross_gram = lax.psum(jnp.dot(own_rows.T, own_rows, precision=HIGH), "space")
        lower_factor = jnp.linalg.cholesky(cross_gram)
        own_basis = lax.linalg.triangular_solve(
            lower_factor, own_rows, left_side=False, lower=True, transpose_a=True
        )
        basis = lax.all_gather(own_basis, "space", axis=0, tiled=True)
    panel = jnp.dot(
        weighted, basis.astype(jnp.bfloat16), preferred_element_type=jnp.float32
    ).astype(jnp.bfloat16)
    row_count = panel.shape[0]
    snap_count = lax.axis_size("snap")
    levels = snap_count.bit_length() - 1
    snap_index = lax.axis_index("snap")
    for level_index in range(levels):
        partner = from_partner(panel, "snap", level_index)
        upper_side = snap_index >> level_index & 1 == 1
        paired = jnp.where(
            upper_side,
            jnp.concatenate([partner, panel], axis=1),
            jnp.concatenate([panel, partner], axis=1),
        )
        merge_index = snap_count - (snap_count >> level_index) + (snap_index >> level_index + 1)
        start_vectors = lax.dynamic_index_in_dim(merge_starts, merge_index, 0, keepdims=True)
        panel = merge_level(paired[None], start_vectors, lambda grams: lax.psum(grams, "space"))[0]
    own_count = row_count // snap_count
    return lax.dynamic_slice_in_dim(panel, lax.axis_index("snap") * own_count, own_count, 0)


def solution(mesh):
    return jax.shard_map(
        local,
        mesh=mesh,
        in_specs=(
            P("space", ("groups", "snap")),
            P("space", None, None, None),
            P("space", None),
            P("space"),
            P(("groups", "snap"), None),
            P(),
        ),
        out_specs=P(("space", "snap"), "groups"),
        check_vma=False,
    )
```

profile of v0, /device:TPU:0, one launch (start us, length us, event | category | flops | bytes accessed | tf_op | source)
XLA Modules:
  0.0 404.1 jit_solution(3854561859859952398)
XLA Ops:
  6.5 0.8 compare_and_fusion.3
  7.4 5.0 %gather_fusion.2 = bf16[32,128,512]{2,1,0:T(8,128)(2,1)} fusion(bf16[32,128,512]{2,1,0:T(8,128)(2,1)} %bitcast.131, s32[1024]{0:T(1024)S(1)} %pad_clamp_fusion.1), kind=kCustom, calls=%fused_computation.2.clone | custom fusion | bytes 8388736 | tf_op jit(solution)/shard_map/jit(_take)/gather | solution.py:36
  12.4 5.0 %gather_fusion.1 = bf16[32,128,512]{2,1,0:T(8,128)(2,1)} fusion(bf16[32,128,512]{2,1,0:T(8,128)(2,1)} %bitcast.132, s32[1024]{0:T(1024)S(1)} %pad_clamp_fusion.2), kind=kCustom, calls=%fused_computation.1.clone | custom fusion | bytes 8388736 | tf_op jit(solution)/shard_map/jit(_take)/gather | solution.py:36
  17.4 4.9 %gather_fusion.3 = bf16[32,128,512]{2,1,0:T(8,128)(2,1)} fusion(bf16[32,128,512]{2,1,0:T(8,128)(2,1)} %bitcast.133, s32[1024]{0:T(1024)S(1)} %pad_clamp_fusion), kind=kCustom, calls=%fused_computation.3.clone | custom fusion | bytes 8388736 | tf_op jit(solution)/shard_map/jit(_take)/gather | solution.py:36
  22.3 5.0 %gather_fusion = bf16[32,128,512]{2,1,0:T(8,128)(2,1)} fusion(bf16[32,128,512]{2,1,0:T(8,128)(2,1)} %bitcast.134, s32[1024]{0:T(1024)S(1)} %pad_clamp_fusion.3), kind=kCustom, calls=%fused_computation.clone | custom fusion | bytes 8388736 | tf_op jit(solution)/shard_map/jit(_take)/gather | solution.py:36
  27.3 7.2 %fusion.2 = f32[32,128,512]{2,1,0:T(8,128)} fusion(bf16[32,128,512]{2,1,0:T(8,128)(2,1)} %gather_fusion.2, pred[32]{0:T(512)(128)(4,1)S(1)} %get-tuple-element.22, bf16[32,4,128,128]{3,2,1,0:T(8,128)(2,1)} %param.15, pred[32]{0:T(512)(128)(4,1)S(1)} %get-tuple-element.28), kind=kOutput, calls=%fused_computation.9 | convolution fusion | flops 539492352 | bytes 13631552 | tf_op jit(solution)/shard_map/bij,bjs->bis/dot_general | solution.py:37
  34.5 4.5 %fusion.4 = f32[32,128,512]{2,1,0:T(8,128)} fusion(bf16[32,128,512]{2,1,0:T(8,128)(2,1)S(1)} %copy-done.2, pred[32]{0:T(512)(128)(4,1)S(1)} %get-tuple-element.18, bf16[32,4,128,128]{3,2,1,0:T(8,128)(2,1)S(1)} %copy-done.4, pred[32]{0:T(512)(128)(4,1)S(1)} %get-tuple-element.30), kind=kOutput, calls=%fused_computation.11 | convolution fusion | flops 539492352 | bytes 13632512 | tf_op jit(solution)/shard_map/bij,bjs->bis/dot_general | solution.py:37
  39.0 4.5 %fusion = f32[32,128,512]{2,1,0:T(8,128)} fusion(bf16[32,128,512]{2,1,0:T(8,128)(2,1)S(1)} %copy-done.3, pred[32]{0:T(512)(128)(4,1)S(1)} %get-tuple-element.20, bf16[32,4,128,128]{3,2,1,0:T(8,128)(2,1)S(1)} %copy-done.4, pred[32]{0:T(512)(128)(4,1)S(1)} %get-tuple-element.29), kind=kOutput, calls=%fused_computation.7 | convolution fusion | flops 539492352 | bytes 13632512 | tf_op jit(solution)/shard_map/bij,bjs->bis/dot_general | solution.py:37
  43.5 11.6 %add_convert_fusion = bf16[32,128,512]{2,1,0:T(8,128)(2,1)S(1)} fusion(f32[32,128,512]{2,1,0:T(8,128)} %fusion, f32[32,128,512]{2,1,0:T(8,128)} %fusion.2, f32[32,128,512]{2,1,0:T(8,128)} %fusion.4, bf16[32,128,512]{2,1,0:T(8,128)(2,1)} %gather_fusion, pred[32]{0:T(512)(128)(4,1)S(1)} %get-tuple-element.6, bf16[32,4,128,128]{3,2,1,0:T(8,128)(2,1)} %param.15, ...), kind=kOutput, calls=%fused_computation.4 | convolution fusion | flops 547880960 | bytes 34603072 | tf_op jit(solution)/shard_map/bij,bjs->bis/dot_general | solution.py:37
  55.2 1.9 copy-done.1
  57.1 3.3 convolution_bitcast_fusion
  60.5 30.1 %reduce-scatter.2.cloned.1.call-done = f32[128,512]{1,0:T(8,128)} async-done(((f32[512,512]{1,0:T(8,128)}), f32[128,512]{1,0:T(8,128)}) %reduce-scatter.2.cloned.1.call-update) | async-done | bytes 262160 | tf_op jit(solution)/shard_map/reduce_scatter | solution.py:56
  90.6 1.3 fusion.72
  91.9 0.9 fusion.73
  93.1 32.7 %all-reduce.5.cloned.1.call-done = f32[128,128]{0,1:T(8,128)} async-done(((f32[128,128]{0,1:T(8,128)}), f32[128,128]{0,1:T(8,128)}) %all-reduce.5.cloned.1.call-update) | async-done | bytes 65552 | tf_op jit(solution)/shard_map/psum | solution.py:66
  125.9 0.9 copy.12
  126.8 0.9 fusion.55
  127.6 11.7 %cholesky.84 = f32[128,128]{1,0:T(8,128)S(1)} custom-call(f32[128,128]{1,0:T(8,128)S(1)} %fusion.55), custom_call_target="Cholesky" | custom-call | tf_op jit(solution)/shard_map/jit(cholesky)/cholesky | solution.py:67
  140.0 0.7 fusion.44
  140.7 9.8 %custom-call.14 = f32[1,128,128]{1,2,0:T(8,128)S(1)} custom-call(f32[1,128,128]{2,1,0:T(8,128)S(1)} %fusion.44), custom_call_target="InvertDiagBlocksLowerTriangular" | custom-call | tf_op jit(solution)/shard_map/triangular_solve/custom-call.2 | solution.py:68
  150.8 14.4 %all_gather.6 = f32[512,128]{0,1:T(8,128)S(1)} all-gather(f32[128,128]{0,1:T(8,128)S(1)} %convolution_bitcast_fusion.4), channel_id=1, replica_groups=mesh['groups'=2,'snap'=4,'space'=4] {'space'}, dimensions={0}, use_global_device_ids=true | all-gather | bytes 327680 | tf_op jit(solution)/shard_map/all_gather | solution.py:71
  165.2 1.3 fusion.74
  166.5 0.9 fusion.75
  167.7 33.3 %all-reduce.7.cloned.1.call-done = f32[128,128]{0,1:T(8,128)} async-done(((f32[128,128]{0,1:T(8,128)}), f32[128,128]{0,1:T(8,128)}) %all-reduce.7.cloned.1.call-update) | async-done | bytes 65552 | tf_op jit(solution)/shard_map/psum | solution.py:66
  201.1 0.9 copy.14
  202.0 0.9 fusion.53
  202.9 11.7 %cholesky.95 = f32[128,128]{1,0:T(8,128)S(1)} custom-call(f32[128,128]{1,0:T(8,128)S(1)} %fusion.53), custom_call_target="Cholesky" | custom-call | tf_op jit(solution)/shard_map/jit(cholesky)/cholesky | solution.py:67
  215.3 0.7 fusion.45
  215.9 9.8 %custom-call.15 = f32[1,128,128]{1,2,0:T(8,128)S(1)} custom-call(f32[1,128,128]{2,1,0:T(8,128)S(1)} %fusion.45), custom_call_target="InvertDiagBlocksLowerTriangular" | custom-call | tf_op jit(solution)/shard_map/triangular_solve/custom-call.2 | solution.py:68
  226.0 12.3 %all_gather.7 = bf16[512,128]{0,1:T(8,128)(2,1)S(1)} all-gather(bf16[128,128]{0,1:T(8,128)(2,1)S(1)} %convolution_bitcast_fusion.3), channel_id=1, replica_groups=mesh['groups'=2,'snap'=4,'space'=4] {'space'}, dimensions={0}, use_global_device_ids=true | all-gather | bytes 163840 | tf_op jit(solution)/shard_map/all_gather | solution.py:71
  238.3 3.7 convolution_convert_fusion.1
  242.1 2.6 collective-permute-done
  244.7 1.8 fusion.34
  246.9 34.0 %all-reduce.9.cloned.1.call-done = f32[256,256]{1,0:T(8,128)} async-done(((f32[256,256]{1,0:T(8,128)}), f32[256,256]{1,0:T(8,128)}) %all-reduce.9.cloned.1.call-update) | async-done | bytes 262160 | tf_op jit(solution)/shard_map/psum | solution.py:89
  280.8 1.3 fusion.39
  282.7 11.7 %custom-call.16 = f32[1,128,128]{2,1,0:T(8,128)S(1)} custom-call(f32[1,128,128]{2,1,0:T(8,128)S(1)} %fusion.49), custom_call_target="Cholesky" | custom-call | tf_op jit(solution)/shard_map/vmap(jit(cholesky))/cholesky | solution.py:21
  295.1 0.7 fusion.46
  295.7 9.8 %custom-call.17 = f32[1,1,128,128]{2,3,1,0:T(8,128)S(1)} custom-call(f32[1,1,128,128]{3,2,1,0:T(8,128)S(1)} %fusion.46), custom_call_target="InvertDiagBlocksLowerTriangular" | custom-call | tf_op jit(solution)/shard_map/vmap()/triangular_solve/custom-call.3 | solution.py:22
  305.9 2.4 convolution_convert_fusion
  308.2 1.5 collective-permute-start.1
  309.8 21.3 %collective-permute-done.1 = bf16[4096,128]{0,1:T(8,128)(2,1)S(1)} collective-permute-done((bf16[4096,128]{0,1:T(8,128)(2,1)S(1)}, bf16[4096,128]{0,1:T(8,128)(2,1)S(1)}, u32[]{:S(2)}, u32[]{:S(2)}) %collective-permute-start.1) | collective-permute-done | bytes 1048608 | tf_op jit(solution)/shard_map/ppermute | solution.py:16
  331.1 1.8 fusion.36
  333.0 35.6 %all-reduce.11.cloned.1.call-done = f32[256,256]{1,0:T(8,128)} async-done(((f32[256,256]{1,0:T(8,128)}), f32[256,256]{1,0:T(8,128)}) %all-reduce.11.cloned.1.call-update) | async-done | bytes 262160 | tf_op jit(solution)/shard_map/psum | solution.py:89
  368.6 1.3 fusion.37
  370.4 12.0 %custom-call.18 = f32[1,128,128]{2,1,0:T(8,128)S(1)} custom-call(f32[1,128,128]{2,1,0:T(8,128)S(1)} %fusion.48), custom_call_target="Cholesky" | custom-call | tf_op jit(solution)/shard_map/vmap(jit(cholesky))/cholesky | solution.py:21
  383.8 9.8 %custom-call.19 = f32[1,1,128,128]{2,3,1,0:T(8,128)S(1)} custom-call(f32[1,1,128,128]{3,2,1,0:T(8,128)S(1)} %fusion.47), custom_call_target="InvertDiagBlocksLowerTriangular" | custom-call | tf_op jit(solution)/shard_map/vmap()/triangular_solve/custom-call.3 | solution.py:22
  393.9 2.4 fusion.35
  396.3 0.7 dynamic-slice_convert_fusion
  (49 shorter events, 6.5 us)
Async XLA Ops:
  6.5 274.3 %copy-start = (f32[3,256,128]{2,1,0:T(8,128)S(1)}, f32[3,256,128]{2,1,0:T(8,128)}, u32[]{:S(2)}) copy-start(f32[3,256,128]{2,1,0:T(8,128)} %param.19) | copy-start | bytes 1179652
  6.5 84.1 %reduce-scatter.2.cloned.1.call-start = ((), (), s32[]{:S(2)}) async-start(), calls=%async_computation.1 | async-start | bytes 1310720 | tf_op jit(solution)/shard_map/reduce_scatter | solution.py:56
  27.3 7.2 %copy-start.2 = (bf16[32,128,512]{2,1,0:T(8,128)(2,1)S(1)}, bf16[32,128,512]{2,1,0:T(8,128)(2,1)}, u32[]{:S(2)}) copy-start(bf16[32,128,512]{2,1,0:T(8,128)(2,1)} %gather_fusion.1) | copy-start | bytes 12582916
  27.3 7.2 %copy-start.4 = (bf16[32,4,128,128]{3,2,1,0:T(8,128)(2,1)S(1)}, bf16[32,4,128,128]{3,2,1,0:T(8,128)(2,1)}, u32[]{:S(2)}) copy-start(bf16[32,4,128,128]{3,2,1,0:T(8,128)(2,1)} %param.15) | copy-start | bytes 12582916
  34.5 4.5 %copy-start.3 = (bf16[32,128,512]{2,1,0:T(8,128)(2,1)S(1)}, bf16[32,128,512]{2,1,0:T(8,128)(2,1)}, u32[]{:S(2)}) copy-start(bf16[32,128,512]{2,1,0:T(8,128)(2,1)} %gather_fusion.3) | copy-start | bytes 12582916
  55.2 1.9 copy-start.1
  57.1 33.5 %copy-start.5 = (f32[512,128]{1,0:T(8,128)S(1)}, f32[512,128]{1,0:T(8,128)}, u32[]{:S(2)}) copy-start(f32[512,128]{1,0:T(8,128)} %param.18) | copy-start | bytes 786436
  60.4 65.4 %all-reduce.5.cloned.1.call-start = ((), (), s32[]{:S(2)}) async-start(), calls=%async_computation.2 | async-start | bytes 131072 | tf_op jit(solution)/shard_map/psum | solution.py:66
  92.9 108.2 %all-reduce.7.cloned.1.call-start = ((), (), s32[]{:S(2)}) async-start(), calls=%async_computation.3 | async-start | bytes 131072 | tf_op jit(solution)/shard_map/psum | solution.py:66
  167.5 113.3 %all-reduce.9.cloned.1.call-start = ((), (), s32[]{:S(2)}) async-start(), calls=%async_computation.4 | async-start | bytes 524288 | tf_op jit(solution)/shard_map/psum | solution.py:89
  242.0 2.7 collective-permute-start
  244.7 1.8 copy-start.7
  246.6 122.0 %all-reduce.11.cloned.1.call-start = ((), (), s32[]{:S(2)}) async-start(), calls=%async_computation.5 | async-start | bytes 524288 | tf_op jit(solution)/shard_map/psum | solution.py:89
  308.2 22.9 %collective-permute-start.1 = (bf16[4096,128]{0,1:T(8,128)(2,1)S(1)}, bf16[4096,128]{0,1:T(8,128)(2,1)S(1)}, u32[]{:S(2)}, u32[]{:S(2)}) collective-permute-start(bf16[4096,128]{0,1:T(8,128)(2,1)S(1)} %convolution_convert_fusion), channel_id=1, source_target_pairs={{0,8},{8,0},{4,12},{12,4},{1,9},{9,1},{5,13},{13,5},{2,10},{10,2},... | collective-permute-start | bytes 3145736 | tf_op jit(solution)/shard_map/ppermute | solution.py:16
  331.1 1.8 copy-start.6
Sparse Core Ops, SparseCore 0:
  60.6 29.9 reduce-scatter.1
  93.0 32.7 all-reduce.4
  167.6 33.4 all-reduce.6
  246.7 34.0 all-reduce.8
  333.1 35.4 all-reduce.10
where the time goes:
time: 411 us; the launch traced here: 404 us
  waiting for transfers between devices  190 us (46%)
  other arithmetic  94.3 us (23%)
  matrix products  52.4 us (13%)
  blocking collectives  26.7 us (6%)
  local copies, waits for them, and re-layouts  24.5 us (6%)
  between operations  13.9 us (3%)
    psum x2, waiting for transfers between devices, local(): lax.psum(grams, 'space')  69.6 us
    psum x2, waiting for transfers between devices, local(): lax.psum(jnp.dot(own_rows.T, own_rows, precision=HIGH), 'space')  66.1 us
    reduce_scatter x1, waiting for transfers between devices, local(): lax.psum_scatter(lax.dot_general(weighted, weighted, (((0,), (0,)), ((),...  30.1 us
    dot_general x4, matrix products, weigh(): jnp.einsum('bij,bjs->bis', factor, source, preferred_element_type=jnp.flo...  27.9 us
    all_gather x2, blocking collectives, local(): basis = lax.all_gather(own_basis, 'space', axis=0, tiled=True)  26.7 us
    another operation x6, other arithmetic, orthonormal(): lower_factor = jnp.linalg.cholesky(cross_gram)  25 us
    another operation x6, other arithmetic, local(): lower_factor = jnp.linalg.cholesky(cross_gram)  24.8 us
    ppermute x2, waiting for transfers between devices, from_partner(): return lax.ppermute(block, axis, route)  24 us
  transfers between devices with their start and end apart: 7, of which 7 were waited for; matrix products, arithmetic and copies ran while one was open for 0% of the time, Pallas kernels for 0%

commit v1 on v0

v1 whole, which is shorter than its diff:
```python
import functools

import jax
import jax.numpy as jnp
from jax import lax
from jax.experimental import pallas as pl
from jax.experimental.pallas import tpu as pltpu
from jax.sharding import PartitionSpec as P

HIGH = lax.Precision.HIGHEST
MESH = pl.DeviceIdType.MESH
F32 = jnp.float32
BF16 = jnp.bfloat16
VMEM = pl.BlockSpec(memory_space=pltpu.VMEM)
ROWS_IN_STEP = 8
TN = (((0,), (0,)), ((), ()))
NT = (((1,), (1,)), ((), ()))


def dot(a, b, dims=(((1,), (0,)), ((), ())), precision=None):
    return lax.dot_general(a, b, dims, precision=precision, preferred_element_type=F32)


def upper_blocks(count):
    return [(i, j) for i in range(count) for j in range(i, count)]


def weigh_kernel(cols_ref, counts_ref, snaps_ref, blocks_ref, weighted_ref, tri_ref, gram):
    step = pl.program_id(0)
    in_step, slots, width, _ = blocks_ref.shape
    for i in range(in_step):
        row = step * in_step + i
        count = counts_ref[row]
        factors = []
        sources = []
        for slot in range(slots):
            factor = blocks_ref[i, slot]
            factors.append(jnp.where(slot < count, factor, jnp.zeros_like(factor)))
            start = pl.multiple_of(cols_ref[row, slot] * width, width)
            sources.append(snaps_ref[pl.ds(start, width), :])
        product = dot(jnp.concatenate(factors, axis=1), jnp.concatenate(sources, axis=0))
        weighted_ref[i * width : (i + 1) * width, :] = product.astype(BF16)
    size = gram.shape[0]
    tall = 256

    @pl.when(step == 0)
    def _():
        gram[...] = jnp.zeros_like(gram)

    for low in range(0, size, tall):
        gram[low : low + tall, low:] += dot(
            weighted_ref[:, low : low + tall], weighted_ref[:, low:], TN
        )

    @pl.when(step == pl.num_programs(0) - 1)
    def _():
        for index, (i, j) in enumerate(upper_blocks(size // 128)):
            tri_ref[index] = gram[i * 128 : (i + 1) * 128, j * 128 : (j + 1) * 128]


def weigh(snapshots, factor_blocks, factor_cols, factor_counts):
    rows, size = snapshots.shape
    row_blocks, slots, width, _ = factor_blocks.shape
    in_step = ROWS_IN_STEP
    count = len(upper_blocks(size // 128))
    return pl.pallas_call(
        weigh_kernel,
        grid=(row_blocks // in_step,),
        in_specs=[
            pl.BlockSpec(memory_space=pltpu.SMEM),
            pl.BlockSpec(memory_space=pltpu.SMEM),
            pl.BlockSpec((rows, size), lambda s: (0, 0)),
            pl.BlockSpec((in_step, slots, width, width), lambda s: (s, 0, 0, 0)),
        ],
        out_specs=[
            pl.BlockSpec((in_step * width, size), lambda s: (s, 0)),
            pl.BlockSpec((count, 128, 128), lambda s: (0, 0, 0)),
        ],
        out_shape=[
            jax.ShapeDtypeStruct((rows, size), BF16),
            jax.ShapeDtypeStruct((count, 128, 128), F32),
        ],
        scratch_shapes=[pltpu.VMEM((size, size), F32)],
        name="weigh",
    )(factor_cols, factor_counts, snapshots, factor_blocks)


def line_kernel(n, own, total, pre_in, pre_out, suf_in, suf_out, sems):
    me = lax.axis_index("space")
    has_left = me > 0
    has_right = me < n - 1
    barrier = pltpu.get_barrier_semaphore()

    @pl.when(has_left)
    def _():
        pl.semaphore_signal(barrier, inc=1, device_id={"space": me - 1}, device_id_type=MESH)

    @pl.when(has_right)
    def _():
        pl.semaphore_signal(barrier, inc=1, device_id={"space": me + 1}, device_id_type=MESH)

    pl.semaphore_wait(barrier, has_left.astype(jnp.int32) + has_right.astype(jnp.int32))

    chunks = own.shape[0]

    def copy(kind, c, other):
        source, target = ((pre_out, pre_in), (suf_out, suf_in))[kind]
        return pltpu.make_async_remote_copy(
            src_ref=source.at[c],
            dst_ref=target.at[c],
            send_sem=sems.at[2 * kind, c],
            recv_sem=sems.at[2 * kind + 1, c],
            device_id={"space": other},
            device_id_type=MESH,
        )

    for c in range(chunks):
        for kind, has_from, has_to, to, out, arrived in (
            (0, has_left, has_right, me + 1, pre_out, pre_in),
            (1, has_right, has_left, me - 1, suf_out, suf_in),
        ):

            @pl.when(has_from)
            def _():
                copy(kind, c, me).wait_recv()

            @pl.when(jnp.logical_and(has_to, has_from))
            def _():
                out[c] = (own[c] + arrived[c].astype(F32)).astype(BF16)

            @pl.when(jnp.logical_and(has_to, jnp.logical_not(has_from)))
            def _():
                out[c] = own[c].astype(BF16)

            @pl.when(has_to)
            def _():
                copy(kind, c, to).start()

    for c in range(chunks):
        total[c] = own[c]

    @pl.when(has_left)
    def _():
        for c in range(chunks):
            total[c] += pre_in[c].astype(F32)

    @pl.when(has_right)
    def _():
        for c in range(chunks):
            total[c] += suf_in[c].astype(F32)

    for c in range(chunks):

        @pl.when(has_right)
        def _():
            copy(0, c, me).wait_send()

        @pl.when(has_left)
        def _():
            copy(1, c, me).wait_send()


def sum_over_space(blocks):
    n = lax.axis_size("space")
    return pl.pallas_call(
        functools.partial(line_kernel, n),
        in_specs=[VMEM],
        out_specs=VMEM,
        out_shape=jax.ShapeDtypeStruct(blocks.shape, F32),
        scratch_shapes=[pltpu.VMEM(blocks.shape, BF16)] * 4
        + [pltpu.SemaphoreType.DMA((4, blocks.shape[0]))],
        compiler_params=pltpu.CompilerParams(collective_id=0, has_side_effects=True),
        name="line_sum",
    )(blocks)


def eliminate(a, e, lane):
    a, e = list(a), list(e)
    groups = len(a)
    row = lax.broadcasted_iota(jnp.int32, (8, 128), 0)
    scale = [jnp.zeros((8, 128), F32)] * groups
    for g in range(groups):
        cols = {
            h: [
                jnp.broadcast_to(a[h][:, lane + 8 * g + k : lane + 8 * g + k + 1], (8, 128))
                for k in range(8)
            ]
            for h in range(g, groups)
        }
        for k in range(8):
            pivot = jnp.broadcast_to(cols[g][k][k : k + 1, :], (8, 128))
            inverse = 1.0 / pivot
            scale[g] = jnp.where(row == k, lax.rsqrt(pivot), scale[g])
            a_row = jnp.broadcast_to(a[g][k : k + 1, :], (8, 128))
            e_row = jnp.broadcast_to(e[g][k : k + 1, :], (8, 128))
            heads = {
                m: jnp.broadcast_to(cols[g][m][k : k + 1, :], (8, 128)) for m in range(k + 1, 8)
            }
            for h in range(g, groups):
                if h == g and k == 7:
                    continue
                f = cols[h][k] * inverse
                if h == g:
                    f = jnp.where(row > k, f, 0.0)
                for m in range(k + 1, 8):
                    cols[h][m] = cols[h][m] - f * heads[m]
                a[h] = a[h] - f * a_row
                e[h] = e[h] - f * e_row
    return [x * s for x, s in zip(a, scale)], [x * s for x, s in zip(e, scale)]


def inverse_factor(cross):
    size = cross.shape[0]
    row = lax.broadcasted_iota(jnp.int32, (size, size), 0)
    col = lax.broadcasted_iota(jnp.int32, (size, size), 1)
    both = jnp.concatenate([cross, (row == col).astype(F32)], axis=1)
    done = []
    for p in range(size // 32):
        rows = [both[p * 32 + 8 * g : p * 32 + 8 * g + 8] for g in range(4)]
        a, e = eliminate([r[:, :size] for r in rows], [r[:, size:] for r in rows], p * 32)
        a, e = jnp.concatenate(a, axis=0), jnp.concatenate(e, axis=0)
        done.append(e)
        if p < size // 32 - 1:
            both = both - dot(a, jnp.concatenate([a, e], axis=1), TN, HIGH)
    return jnp.concatenate(done, axis=0)


def orthonormal(z):
    return dot(z, inverse_factor(dot(z, z, TN, HIGH)), NT, HIGH)


def compress_kernel(tri_ref, start_ref, weighted_ref, panel_ref, diag_ref, gram, basis):
    size = gram.shape[0]
    for index, (i, j) in enumerate(upper_blocks(size // 128)):
        block = tri_ref[index]
        gram[i * 128 : (i + 1) * 128, j * 128 : (j + 1) * 128] = block
        if i != j:
            gram[j * 128 : (j + 1) * 128, i * 128 : (i + 1) * 128] = block.T
    basis[...] = start_ref[...]

    def sweep(_, carry):
        basis[...] = orthonormal(dot(gram[...], basis[...], precision=HIGH))
        return carry

    lax.fori_loop(0, 2, sweep, 0)
    rounded = basis[...].astype(BF16)
    tall = 1024
    for low in range(0, weighted_ref.shape[0], tall):
        panel_ref[low : low + tall, :] = dot(weighted_ref[low : low + tall, :], rounded).astype(BF16)
    wide = rounded.astype(F32)
    diag_ref[...] = dot(wide, dot(gram[...], wide, precision=HIGH), TN, HIGH)


def compress(tri, start_basis, weighted):
    size, modes = start_basis.shape
    return pl.pallas_call(
        compress_kernel,
        in_specs=[VMEM] * 3,
        out_specs=[VMEM] * 2,
        out_shape=[
            jax.ShapeDtypeStruct((weighted.shape[0], modes), BF16),
            jax.ShapeDtypeStruct((modes, modes), F32),
        ],
        scratch_shapes=[pltpu.VMEM((size, size), F32), pltpu.VMEM((size, modes), F32)],
        name="compress",
    )(tri, start_basis, weighted)


def flipped(index, bit):
    return index + (1 - 2 * (index // (1 << bit) % 2)) * (1 << bit)


def pair_kernel(
    n, level, panel, diag, pair, cross_gram, got, got_diag, out, came, z_out, z_came, sems, x_sems, z_sems
):
    snap = lax.axis_index("snap")
    space = lax.axis_index("space")
    bit = snap // (1 << level) % 2
    partner = flipped(snap, level)
    half, _, rows, modes = panel.shape
    barrier = pltpu.get_barrier_semaphore()
    for b in range(level + 1):
        pl.semaphore_signal(
            barrier, inc=1, device_id={"snap": flipped(snap, b)}, device_id_type=MESH
        )
    for k in range(1, n):
        pl.semaphore_signal(
            barrier, inc=1, device_id={"space": lax.rem(space + k, n)}, device_id_type=MESH
        )
    pl.semaphore_wait(barrier, level + n)

    def remote(source, target, send, recv, device):
        return pltpu.make_async_remote_copy(
            src_ref=source,
            dst_ref=target,
            send_sem=send,
            recv_sem=recv,
            device_id=device,
            device_id_type=MESH,
        )

    copies = [
        remote(panel.at[h, 1 - bit], got.at[h], sems.at[0, h], sems.at[1, h], {"snap": partner})
        for h in range(half)
    ]
    copies.append(
        remote(diag, got_diag, sems.at[0, half], sems.at[1, half], {"snap": partner})
    )
    for c in copies:
        c.start()
    cross = jnp.zeros((modes, modes), F32)
    upper = bit == 1
    for h in range(half):
        copies[h].wait_recv()
        mine, theirs = panel[h, bit], got[h]
        left = jnp.where(upper, theirs, mine)
        right = jnp.where(upper, mine, theirs)
        pair[h * rows : (h + 1) * rows, :modes] = left
        pair[h * rows : (h + 1) * rows, modes:] = right
        cross = cross + dot(left, right, TN)
    for b in range(level + 1):
        out[b] = cross
        step = remote(
            out.at[b], came.at[b], x_sems.at[0, b], x_sems.at[1, b], {"snap": flipped(snap, b)}
        )
        step.start()
        step.wait_recv()
        cross = cross + came[b]
        copies.append(step)
    z_out[...] = cross.astype(BF16)
    steps = [
        remote(
            z_out,
            z_came.at[k - 1],
            z_sems.at[0, k - 1],
            z_sems.at[1, k - 1],
            {"space": lax.rem(space + k, n)},
        )
        for k in range(1, n)
    ]
    for s in steps:
        s.start()
    copies[half].wait_recv()
    cross_gram[:modes, :modes] = jnp.where(upper, got_diag[...], diag[...])
    cross_gram[modes:, modes:] = jnp.where(upper, diag[...], got_diag[...])
    for k, s in enumerate(steps):
        s.wait_recv()
        cross = cross + z_came[k].astype(F32)
    cross_gram[:modes, modes:] = cross
    cross_gram[modes:, :modes] = cross.T
    for c in copies + steps:
        c.wait_send()


def pair_up(panel, diag, level, parts):
    n = lax.axis_size("space")
    rows, modes = panel.shape
    half = parts // 2
    rows_in = rows // parts
    return pl.pallas_call(
        functools.partial(pair_kernel, n, level),
        in_specs=[VMEM] * 2,
        out_specs=[VMEM] * 2,
        out_shape=[
            jax.ShapeDtypeStruct((rows // 2, 2 * modes), BF16),
            jax.ShapeDtypeStruct((2 * modes, 2 * modes), F32),
        ],
        scratch_shapes=[
            pltpu.VMEM((half, rows_in, modes), BF16),
            pltpu.VMEM((modes, modes), F32),
            pltpu.VMEM((level + 1, modes, modes), F32),
            pltpu.VMEM((level + 1, modes, modes), F32),
            pltpu.VMEM((modes, modes), BF16),
            pltpu.VMEM((n - 1, modes, modes), BF16),
            pltpu.SemaphoreType.DMA((2, half + 1)),
            pltpu.SemaphoreType.DMA((2, level + 1)),
            pltpu.SemaphoreType.DMA((2, n - 1)),
        ],
        compiler_params=pltpu.CompilerParams(collective_id=1 + level, has_side_effects=True),
        name="pair_up",
    )(panel.reshape(half, 2, rows_in, modes), diag)


def mix_kernel(snap_count, level, pair, cross_gram, starts, *outs):
    snap = lax.axis_index("snap")
    index = snap_count - (snap_count >> level) + snap // (1 << (level + 1))
    steered = dot(cross_gram[...], starts[index], precision=HIGH)
    mixing = orthonormal(steered).astype(BF16)
    outs[0][...] = dot(pair[...], mixing).astype(BF16)
    if len(outs) > 1:
        wide = mixing.astype(F32)
        outs[1][...] = dot(wide, dot(cross_gram[...], wide, precision=HIGH), TN, HIGH)


def mix(pair, cross_gram, merge_starts, level, snap_count, last):
    rows = pair.shape[0]
    modes = merge_starts.shape[2]
    shapes = [jax.ShapeDtypeStruct((rows, modes), BF16)]
    if not last:
        shapes.append(jax.ShapeDtypeStruct((modes, modes), F32))
    return pl.pallas_call(
        functools.partial(mix_kernel, snap_count, level),
        in_specs=[VMEM] * 3,
        out_specs=[VMEM] * len(shapes),
        out_shape=shapes,
        name="mix",
    )(pair, cross_gram, merge_starts)


def local(snapshots, factor_blocks, factor_cols, factor_counts, start_basis, merge_starts):
    weighted, tri = weigh(snapshots, factor_blocks, factor_cols, factor_counts)
    tri = sum_over_space(tri)
    panel, diag = compress(tri, start_basis, weighted)
    parts = lax.axis_size("snap")
    snap_count = parts
    levels = snap_count.bit_length() - 1
    for level in range(levels):
        pair, cross_gram = pair_up(panel, diag, level, parts)
        parts //= 2
        last = level == levels - 1
        made = mix(pair, cross_gram, merge_starts, level, snap_count, last)
        panel = made[0]
        diag = None if last else made[1]
    return panel


def solution(mesh):
    return jax.shard_map(
        local,
        mesh=mesh,
        in_specs=(
            P("space", ("groups", "snap")),
            P("space", None, None, None),
            P("space", None),
            P("space"),
            P(("groups", "snap"), None),
            P(),
        ),
        out_specs=P(("space", "snap"), "groups"),
        check_vma=False,
    )
```

time: 411 us -> 258 us (0.63); the launches traced: 404 us -> 258 us
  Pallas kernels: 0 us -> 257 us
  waiting for transfers between devices: 190 us -> 0 us
  other arithmetic: 94.3 us -> 0 us
  matrix products: 52.4 us -> 0 us
  blocking collectives: 26.7 us -> 0 us
  local copies, waits for them, and re-layouts: 24.5 us -> 1.37 us
  between operations: 13.9 us -> 0.03 us
    pallas_call x0 -> x7, Pallas kernels: none -> 257 us  [the longest x1 180 us: sum_over_space(): pl.pallas_call(functools.partial(line_kernel, n), in_specs=[VMEM], out_sp...]
    psum x4 -> x0, waiting for transfers between devices: 136 us -> none  [the longest x2 69.6 us: local(): lax.psum(grams, 'space')]
    another operation x20 -> x0, other arithmetic: 91.7 us -> none  [the longest x6 25 us: orthonormal(): lower_factor = jnp.linalg.cholesky(cross_gram)]
    dot_general x18 -> x0, matrix products: 51.2 us -> none  [the longest x4 27.9 us: weigh(): jnp.einsum('bij,bjs->bis', factor, source, preferred_element_type=jnp.flo...]
    reduce_scatter x1 -> x0, waiting for transfers between devices: 30.1 us -> none  [local(): lax.psum_scatter(lax.dot_general(weighted, weighted, (((0,), (0,)), ((),...]
    all_gather x2 -> x0, blocking collectives: 26.7 us -> none  [local(): basis = lax.all_gather(own_basis, 'space', axis=0, tiled=True)]
    ppermute x2 -> x0, waiting for transfers between devices: 24 us -> none  [from_partner(): return lax.ppermute(block, axis, route)]
    gather x4 -> x0, local copies, waits for them, and re-layouts: 19.8 us -> none  [weigh(): source = jnp.take(blocks_in, factor_cols[:, slot_index], axis=0)]
  transfers between devices with their start and end apart: 7 -> 0, of which waited for: 7 -> 0; matrix products, arithmetic and copies ran while one was open for 0% -> 0% of each run, Pallas kernels for 0% -> 0%
where the time goes in v1:
time: 258 us
  Pallas kernels  257 us (100%)
    pallas_call x1, Pallas kernels, sum_over_space(): pl.pallas_call(functools.partial(line_kernel, n), in_specs=[VMEM], out_sp...  180 us
    pallas_call x2, Pallas kernels, pair_up(): pl.pallas_call(functools.partial(pair_kernel, n, level), in_specs=[VMEM]...  30.5 us
    pallas_call x1, Pallas kernels, compress(): pl.pallas_call(compress_kernel, in_specs=[VMEM] * 3, out_specs=[VMEM] * 2...  20.1 us
    pallas_call x2, Pallas kernels, mix(): pl.pallas_call(functools.partial(mix_kernel, snap_count, level), in_specs...  16.1 us
    pallas_call x1, Pallas kernels, weigh(): pl.pallas_call(weigh_kernel, grid=(row_blocks // in_step,), in_specs=[pl....  9.56 us

profile of v1, /device:TPU:0, one launch (start us, length us, event | category | flops | bytes accessed | tf_op | source)
XLA Modules:
  0.0 258.1 jit_solution(29005544790020474)
XLA Ops:
  0.0 1.4 copy.7.cols_ref
  1.4 9.6 %weigh.1 = (bf16[4096,512]{1,0:T(8,128)(2,1)}, f32[10,128,128]{2,1,0:T(8,128)}) custom-call(s32[32,4]{1,0:T(8,128)} %copy.7.cols_ref, s32[32]{0:T(128)} %counts_ref.1, bf16[4096,512]{1,0:T(8,128)(2,1)} %snaps_ref.1, bf16[32,4,128,128]{3,2,1,0:T(8,128)(2,1)} %blocks_ref.1), custom_call_target="tpu_custom_call" | custom-call | tf_op jit(solution)/shard_map/weigh/pallas_call | solution.py:66
  10.9 180.4 %line_sum.1.tri_ref = f32[10,128,128]{2,1,0:T(8,128)} custom-call(f32[10,128,128]{2,1,0:T(8,128)} %get-tuple-element.15.own), custom_call_target="tpu_custom_call" | custom-call | tf_op jit(solution)/shard_map/line_sum/pallas_call | solution.py:165
  191.3 20.1 %compress.1 = (bf16[4096,128]{1,0:T(8,128)(2,1)}, f32[128,128]{1,0:T(8,128)}) custom-call(f32[10,128,128]{2,1,0:T(8,128)} %line_sum.1.tri_ref, f32[512,128]{1,0:T(8,128)} %start_ref.1, bf16[4096,512]{1,0:T(8,128)(2,1)} %get-tuple-element.16.weighted_ref), custom_call_target="tpu_custom_call" | custom-call | tf_op jit(solution)/shard_map/compress/pallas_call | solution.py:256
  211.4 11.3 %pair_up.2 = (bf16[2048,256]{1,0:T(8,128)(2,1)}, f32[256,256]{1,0:T(8,128)}) custom-call(bf16[2,2,1024,128]{3,2,1,0:T(8,128)(2,1)} %bitcast.2, f32[128,128]{1,0:T(8,128)} %get-tuple-element.18.diag), custom_call_target="tpu_custom_call" | custom-call | tf_op jit(solution)/shard_map/pair_up/pallas_call | solution.py:360
  222.7 8.4 %mix.2 = (bf16[2048,128]{1,0:T(8,128)(2,1)}, f32[128,128]{1,0:T(8,128)}) custom-call(bf16[2048,256]{1,0:T(8,128)(2,1)} %get-tuple-element.19.pair, f32[256,256]{1,0:T(8,128)} %get-tuple-element.20.cross_gram, f32[3,256,128]{2,1,0:T(8,128)} %starts.3), custom_call_target="tpu_custom_call" | custom-call | tf_op jit(solution)/shard_map/mix/pallas_call | solution.py:401
  231.1 19.2 %pair_up.3 = (bf16[1024,256]{1,0:T(8,128)(2,1)}, f32[256,256]{1,0:T(8,128)}) custom-call(bf16[1,2,1024,128]{3,2,1,0:T(8,128)(2,1)} %bitcast.3, f32[128,128]{1,0:T(8,128)} %get-tuple-element.22.diag), custom_call_target="tpu_custom_call" | custom-call | tf_op jit(solution)/shard_map/pair_up/pallas_call | solution.py:360
  250.3 7.8 %mix.3 = bf16[1024,128]{1,0:T(8,128)(2,1)} custom-call(bf16[1024,256]{1,0:T(8,128)(2,1)} %get-tuple-element.23.pair, f32[256,256]{1,0:T(8,128)} %get-tuple-element.24.cross_gram, f32[3,256,128]{2,1,0:T(8,128)} %starts.3), custom_call_target="tpu_custom_call" | custom-call | tf_op jit(solution)/shard_map/mix/pallas_call | solution.py:401

commit v2 on v1

--- a/solution.py
+++ b/solution.py
@@ -13,6 +13,7 @@
 BF16 = jnp.bfloat16
 VMEM = pl.BlockSpec(memory_space=pltpu.VMEM)
 ROWS_IN_STEP = 8
+LAG = 3
 TN = (((0,), (0,)), ((), ()))
 NT = (((1,), (1,)), ((), ()))
 
@@ -36,7 +37,7 @@
         for slot in range(slots):
             factor = blocks_ref[i, slot]
             factors.append(jnp.where(slot < count, factor, jnp.zeros_like(factor)))
-            start = pl.multiple_of(cols_ref[row, slot] * width, width)
+            start = pl.multiple_of(cols_ref[slot, row] * width, width)
             sources.append(snaps_ref[pl.ds(start, width), :])
         product = dot(jnp.concatenate(factors, axis=1), jnp.concatenate(sources, axis=0))
         weighted_ref[i * width : (i + 1) * width, :] = product.astype(BF16)
@@ -82,7 +83,7 @@
         ],
         scratch_shapes=[pltpu.VMEM((size, size), F32)],
         name="weigh",
-    )(factor_cols, factor_counts, snapshots, factor_blocks)
+    )(factor_cols.T, factor_counts, snapshots, factor_blocks)
 
 
 def line_kernel(n, own, total, pre_in, pre_out, suf_in, suf_out, sems):
@@ -114,27 +115,33 @@
             device_id_type=MESH,
         )
 
-    for c in range(chunks):
-        for kind, has_from, has_to, to, out, arrived in (
-            (0, has_left, has_right, me + 1, pre_out, pre_in),
-            (1, has_right, has_left, me - 1, suf_out, suf_in),
+    def turn(t, carry):
+        for kind, behind, has_from, has_to, to, out, arrived in (
+            (0, me, has_left, has_right, me + 1, pre_out, pre_in),
+            (1, n - 1 - me, has_right, has_left, me - 1, suf_out, suf_in),
         ):
-
-            @pl.when(has_from)
+            c = t - LAG * behind
+            here = jnp.logical_and(c >= 0, c < chunks)
+
+            @pl.when(jnp.logical_and(here, has_from))
             def _():
                 copy(kind, c, me).wait_recv()
 
-            @pl.when(jnp.logical_and(has_to, has_from))
+            @pl.when(jnp.logical_and(here, jnp.logical_and(has_to, has_from)))
             def _():
                 out[c] = (own[c] + arrived[c].astype(F32)).astype(BF16)
 
-            @pl.when(jnp.logical_and(has_to, jnp.logical_not(has_from)))
+            @pl.when(jnp.logical_and(here, jnp.logical_and(has_to, jnp.logical_not(has_from))))
             def _():
                 out[c] = own[c].astype(BF16)
 
-            @pl.when(has_to)
+            @pl.when(jnp.logical_and(here, has_to))
             def _():
                 copy(kind, c, to).start()
+
+        return carry
+
+    lax.fori_loop(0, chunks + LAG * (n - 1), turn, 0)
 
     for c in range(chunks):
         total[c] = own[c]
@@ -271,7 +278,25 @@
 
 
 def pair_kernel(
-    n, level, panel, diag, pair, cross_gram, got, got_diag, out, came, z_out, z_came, sems, x_sems, z_sems
+    n,
+    level,
+    panel,
+    diag,
+    pair,
+    cross_gram,
+    got,
+    got_diag,
+    mine_all,
+    out,
+    came,
+    z_out,
+    z_came,
+    sum_out,
+    sum_came,
+    sems,
+    x_sems,
+    z_sems,
+    s_sems,
 ):
     snap = lax.axis_index("snap")
     space = lax.axis_index("space")
@@ -279,15 +304,23 @@
     partner = flipped(snap, level)
     half, _, rows, modes = panel.shape
     barrier = pltpu.get_barrier_semaphore()
-    for b in range(level + 1):
-        pl.semaphore_signal(
-            barrier, inc=1, device_id={"snap": flipped(snap, b)}, device_id_type=MESH
-        )
+    members = 1 << (level + 1)
+    own = lax.rem(snap, members)
+    share = modes // members
+
+    def member(k):
+        return snap - own + lax.rem(own + k, members)
+
+    def share_of(k):
+        return pl.ds(pl.multiple_of(lax.rem(own + k, members) * share, share), share)
+
+    for k in range(1, members):
+        pl.semaphore_signal(barrier, inc=1, device_id={"snap": member(k)}, device_id_type=MESH)
     for k in range(1, n):
         pl.semaphore_signal(
             barrier, inc=1, device_id={"space": lax.rem(space + k, n)}, device_id_type=MESH
         )
-    pl.semaphore_wait(barrier, level + n)
+    pl.semaphore_wait(barrier, members - 1 + n - 1)
 
     def remote(source, target, send, recv, device):
         return pltpu.make_async_remote_copy(
@@ -318,16 +351,25 @@
         pair[h * rows : (h + 1) * rows, :modes] = left
         pair[h * rows : (h + 1) * rows, modes:] = right
         cross = cross + dot(left, right, TN)
-    for b in range(level + 1):
-        out[b] = cross
-        step = remote(
-            out.at[b], came.at[b], x_sems.at[0, b], x_sems.at[1, b], {"snap": flipped(snap, b)}
-        )
-        step.start()
-        step.wait_recv()
-        cross = cross + came[b]
-        copies.append(step)
-    z_out[...] = cross.astype(BF16)
+    mine_all[...] = cross
+    out[...] = cross.astype(BF16)
+    spread = [
+        remote(
+            out.at[share_of(k)],
+            came.at[k - 1],
+            x_sems.at[0, k - 1],
+            x_sems.at[1, k - 1],
+            {"snap": member(k)},
+        )
+        for k in range(1, members)
+    ]
+    for c in spread:
+        c.start()
+    part = mine_all[share_of(0), :]
+    for k, c in enumerate(spread):
+        c.wait_recv()
+        part = part + came[k].astype(F32)
+    z_out[...] = part.astype(BF16)
     steps = [
         remote(
             z_out,
@@ -345,10 +387,27 @@
     cross_gram[modes:, modes:] = jnp.where(upper, diag[...], got_diag[...])
     for k, s in enumerate(steps):
         s.wait_recv()
-        cross = cross + z_came[k].astype(F32)
-    cross_gram[:modes, modes:] = cross
+        part = part + z_came[k].astype(F32)
+    sum_out[...] = part.astype(BF16)
+    collected = [
+        remote(
+            sum_out,
+            sum_came.at[k - 1],
+            s_sems.at[0, k - 1],
+            s_sems.at[1, k - 1],
+            {"snap": member(k)},
+        )
+        for k in range(1, members)
+    ]
+    for c in collected:
+        c.start()
+    cross_gram[share_of(0), modes:] = part.astype(BF16).astype(F32)
+    for k, c in enumerate(collected):
+        c.wait_recv()
+        cross_gram[share_of(members - 1 - k), modes:] = sum_came[k].astype(F32)
+    cross = cross_gram[:modes, modes:]
     cross_gram[modes:, :modes] = cross.T
-    for c in copies + steps:
+    for c in copies + spread + steps + collected:
         c.wait_send()
 
 
@@ -357,6 +416,8 @@
     rows, modes = panel.shape
     half = parts // 2
     rows_in = rows // parts
+    members = 1 << (level + 1)
+    share = modes // members
     return pl.pallas_call(
         functools.partial(pair_kernel, n, level),
         in_specs=[VMEM] * 2,
@@ -368,13 +429,17 @@
         scratch_shapes=[
             pltpu.VMEM((half, rows_in, modes), BF16),
             pltpu.VMEM((modes, modes), F32),
-            pltpu.VMEM((level + 1, modes, modes), F32),
-            pltpu.VMEM((level + 1, modes, modes), F32),
+            pltpu.VMEM((modes, modes), F32),
             pltpu.VMEM((modes, modes), BF16),
-            pltpu.VMEM((n - 1, modes, modes), BF16),
+            pltpu.VMEM((members - 1, share, modes), BF16),
+            pltpu.VMEM((share, modes), BF16),
+            pltpu.VMEM((n - 1, share, modes), BF16),
+            pltpu.VMEM((share, modes), BF16),
+            pltpu.VMEM((members - 1, share, modes), BF16),
             pltpu.SemaphoreType.DMA((2, half + 1)),
-            pltpu.SemaphoreType.DMA((2, level + 1)),
+            pltpu.SemaphoreType.DMA((2, members - 1)),
             pltpu.SemaphoreType.DMA((2, n - 1)),
+            pltpu.SemaphoreType.DMA((2, members - 1)),
         ],
         compiler_params=pltpu.CompilerParams(collective_id=1 + level, has_side_effects=True),
         name="pair_up",

time: 258 us -> 103 us (0.40)
  Pallas kernels: 257 us -> 103 us
    pallas_call x1, Pallas kernels: 180 us -> 23.4 us  [sum_over_space(): pl.pallas_call(functools.partial(line_kernel, n), in_specs=[VMEM], out_sp...]
    pallas_call x2, Pallas kernels: 30.5 us -> 33.8 us  [pair_up(): pl.pallas_call(functools.partial(pair_kernel, n, level), in_specs=[VMEM]...]
where the time goes in v2:
time: 103 us
  Pallas kernels  103 us (100%)
    pallas_call x2, Pallas kernels, pair_up(): pl.pallas_call(functools.partial(pair_kernel, n, level), in_specs=[VMEM]...  33.8 us
    pallas_call x1, Pallas kernels, sum_over_space(): pl.pallas_call(functools.partial(line_kernel, n), in_specs=[VMEM], out_sp...  23.4 us
    pallas_call x1, Pallas kernels, compress(): pl.pallas_call(compress_kernel, in_specs=[VMEM] * 3, out_specs=[VMEM] * 2...  20.1 us
    pallas_call x2, Pallas kernels, mix(): pl.pallas_call(functools.partial(mix_kernel, snap_count, level), in_specs...  16.1 us
    pallas_call x1, Pallas kernels, weigh(): pl.pallas_call(weigh_kernel, grid=(row_blocks // in_step,), in_specs=[pl....  9.55 us

profile of v2, /device:TPU:0, one launch (start us, length us, event | category | flops | bytes accessed | tf_op | source)
XLA Modules:
  0.0 103.0 jit_solution(12708903947207459253)
XLA Ops:
  0.0 9.6 %weigh.1 = (bf16[4096,512]{1,0:T(8,128)(2,1)}, f32[10,128,128]{2,1,0:T(8,128)}) custom-call(s32[4,32]{1,0:T(4,128)} %bitcast.5, s32[32]{0:T(128)} %counts_ref.1, bf16[4096,512]{1,0:T(8,128)(2,1)} %snaps_ref.1, bf16[32,4,128,128]{3,2,1,0:T(8,128)(2,1)} %blocks_ref.1), custom_call_target="tpu_custom_call" | custom-call | tf_op jit(solution)/shard_map/weigh/pallas_call | solution.py:67
  9.6 23.4 %line_sum.1.tri_ref = f32[10,128,128]{2,1,0:T(8,128)} custom-call(f32[10,128,128]{2,1,0:T(8,128)} %get-tuple-element.15.own), custom_call_target="tpu_custom_call" | custom-call | tf_op jit(solution)/shard_map/line_sum/pallas_call | solution.py:172
  33.0 20.1 %compress.1 = (bf16[4096,128]{1,0:T(8,128)(2,1)}, f32[128,128]{1,0:T(8,128)}) custom-call(f32[10,128,128]{2,1,0:T(8,128)} %line_sum.1.tri_ref, f32[512,128]{1,0:T(8,128)} %start_ref.1, bf16[4096,512]{1,0:T(8,128)(2,1)} %get-tuple-element.16.weighted_ref), custom_call_target="tpu_custom_call" | custom-call | tf_op jit(solution)/shard_map/compress/pallas_call | solution.py:263
  53.0 11.8 %pair_up.2 = (bf16[2048,256]{1,0:T(8,128)(2,1)}, f32[256,256]{1,0:T(8,128)}) custom-call(bf16[2,2,1024,128]{3,2,1,0:T(8,128)(2,1)} %bitcast.3, f32[128,128]{1,0:T(8,128)} %get-tuple-element.18.diag), custom_call_target="tpu_custom_call" | custom-call | tf_op jit(solution)/shard_map/pair_up/pallas_call | solution.py:421
  64.8 8.4 %mix.2 = (bf16[2048,128]{1,0:T(8,128)(2,1)}, f32[128,128]{1,0:T(8,128)}) custom-call(bf16[2048,256]{1,0:T(8,128)(2,1)} %get-tuple-element.19.pair, f32[256,256]{1,0:T(8,128)} %get-tuple-element.20.cross_gram, f32[3,256,128]{2,1,0:T(8,128)} %starts.3), custom_call_target="tpu_custom_call" | custom-call | tf_op jit(solution)/shard_map/mix/pallas_call | solution.py:466
  73.2 22.0 %pair_up.3 = (bf16[1024,256]{1,0:T(8,128)(2,1)}, f32[256,256]{1,0:T(8,128)}) custom-call(bf16[1,2,1024,128]{3,2,1,0:T(8,128)(2,1)} %bitcast.4, f32[128,128]{1,0:T(8,128)} %get-tuple-element.22.diag), custom_call_target="tpu_custom_call" | custom-call | tf_op jit(solution)/shard_map/pair_up/pallas_call | solution.py:421
  95.2 7.8 %mix.3 = bf16[1024,128]{1,0:T(8,128)(2,1)} custom-call(bf16[1024,256]{1,0:T(8,128)(2,1)} %get-tuple-element.23.pair, f32[256,256]{1,0:T(8,128)} %get-tuple-element.24.cross_gram, f32[3,256,128]{2,1,0:T(8,128)} %starts.3), custom_call_target="tpu_custom_call" | custom-call | tf_op jit(solution)/shard_map/mix/pallas_call | solution.py:466

commit v3 on v2

--- a/solution.py
+++ b/solution.py
@@ -86,22 +86,10 @@
     )(factor_cols.T, factor_counts, snapshots, factor_blocks)
 
 
-def line_kernel(n, own, total, pre_in, pre_out, suf_in, suf_out, sems):
+def line_sum(n, own, total, pre_in, pre_out, suf_in, suf_out, sems):
     me = lax.axis_index("space")
     has_left = me > 0
     has_right = me < n - 1
-    barrier = pltpu.get_barrier_semaphore()
-
-    @pl.when(has_left)
-    def _():
-        pl.semaphore_signal(barrier, inc=1, device_id={"space": me - 1}, device_id_type=MESH)
-
-    @pl.when(has_right)
-    def _():
-        pl.semaphore_signal(barrier, inc=1, device_id={"space": me + 1}, device_id_type=MESH)
-
-    pl.semaphore_wait(barrier, has_left.astype(jnp.int32) + has_right.astype(jnp.int32))
-
     chunks = own.shape[0]
 
     def copy(kind, c, other):
@@ -165,20 +153,6 @@
         @pl.when(has_left)
         def _():
             copy(1, c, me).wait_send()
-
-
-def sum_over_space(blocks):
-    n = lax.axis_size("space")
-    return pl.pallas_call(
-        functools.partial(line_kernel, n),
-        in_specs=[VMEM],
-        out_specs=VMEM,
-        out_shape=jax.ShapeDtypeStruct(blocks.shape, F32),
-        scratch_shapes=[pltpu.VMEM(blocks.shape, BF16)] * 4
-        + [pltpu.SemaphoreType.DMA((4, blocks.shape[0]))],
-        compiler_params=pltpu.CompilerParams(collective_id=0, has_side_effects=True),
-        name="line_sum",
-    )(blocks)
 
 
 def eliminate(a, e, lane):
@@ -236,7 +210,7 @@
     return dot(z, inverse_factor(dot(z, z, TN, HIGH)), NT, HIGH)
 
 
-def compress_kernel(tri_ref, start_ref, weighted_ref, panel_ref, diag_ref, gram, basis):
+def compress(tri_ref, start_ref, gram, basis, diag_ref):
     size = gram.shape[0]
     for index, (i, j) in enumerate(upper_blocks(size // 128)):
         block = tri_ref[index]
@@ -251,59 +225,34 @@
 
     lax.fori_loop(0, 2, sweep, 0)
     rounded = basis[...].astype(BF16)
-    tall = 1024
-    for low in range(0, weighted_ref.shape[0], tall):
-        panel_ref[low : low + tall, :] = dot(weighted_ref[low : low + tall, :], rounded).astype(BF16)
     wide = rounded.astype(F32)
     diag_ref[...] = dot(wide, dot(gram[...], wide, precision=HIGH), TN, HIGH)
-
-
-def compress(tri, start_basis, weighted):
-    size, modes = start_basis.shape
-    return pl.pallas_call(
-        compress_kernel,
-        in_specs=[VMEM] * 3,
-        out_specs=[VMEM] * 2,
-        out_shape=[
-            jax.ShapeDtypeStruct((weighted.shape[0], modes), BF16),
-            jax.ShapeDtypeStruct((modes, modes), F32),
-        ],
-        scratch_shapes=[pltpu.VMEM((size, size), F32), pltpu.VMEM((size, modes), F32)],
-        name="compress",
-    )(tri, start_basis, weighted)
+    return rounded
 
 
 def flipped(index, bit):
     return index + (1 - 2 * (index // (1 << bit) % 2)) * (1 << bit)
 
 
-def pair_kernel(
-    n,
-    level,
-    panel,
-    diag,
-    pair,
-    cross_gram,
-    got,
-    got_diag,
-    mine_all,
-    out,
-    came,
-    z_out,
-    z_came,
-    sum_out,
-    sum_came,
-    sems,
-    x_sems,
-    z_sems,
-    s_sems,
-):
+def remote(source, target, send, recv, device):
+    return pltpu.make_async_remote_copy(
+        src_ref=source,
+        dst_ref=target,
+        send_sem=send,
+        recv_sem=recv,
+        device_id=device,
+        device_id_type=MESH,
+    )
+
+
+def pair_up(n, level, make, diag, panel, pair, cross_gram, scratch):
+    (got, got_diag, mine_all, out, came, z_out, z_came, sum_out, sum_came) = scratch[:9]
+    sems, x_sems, z_sems, s_sems = scratch[9:]
     snap = lax.axis_index("snap")
     space = lax.axis_index("space")
     bit = snap // (1 << level) % 2
     partner = flipped(snap, level)
     half, _, rows, modes = panel.shape
-    barrier = pltpu.get_barrier_semaphore()
     members = 1 << (level + 1)
     own = lax.rem(snap, members)
     share = modes // members
@@ -314,33 +263,17 @@
     def share_of(k):
         return pl.ds(pl.multiple_of(lax.rem(own + k, members) * share, share), share)
 
-    for k in range(1, members):
-        pl.semaphore_signal(barrier, inc=1, device_id={"snap": member(k)}, device_id_type=MESH)
-    for k in range(1, n):
-        pl.semaphore_signal(
-            barrier, inc=1, device_id={"space": lax.rem(space + k, n)}, device_id_type=MESH
-        )
-    pl.semaphore_wait(barrier, members - 1 + n - 1)
-
-    def remote(source, target, send, recv, device):
-        return pltpu.make_async_remote_copy(
-            src_ref=source,
-            dst_ref=target,
-            send_sem=send,
-            recv_sem=recv,
-            device_id=device,
-            device_id_type=MESH,
-        )
-
     copies = [
         remote(panel.at[h, 1 - bit], got.at[h], sems.at[0, h], sems.at[1, h], {"snap": partner})
         for h in range(half)
     ]
-    copies.append(
-        remote(diag, got_diag, sems.at[0, half], sems.at[1, half], {"snap": partner})
-    )
-    for c in copies:
-        c.start()
+    copies.append(remote(diag, got_diag, sems.at[0, half], sems.at[1, half], {"snap": partner}))
+    for h in range(half):
+        panel[h, 1 - bit] = make(h, 1 - bit)
+        copies[h].start()
+    copies[half].start()
+    for h in range(half):
+        panel[h, bit] = make(h, bit)
     cross = jnp.zeros((modes, modes), F32)
     upper = bit == 1
     for h in range(half):
@@ -411,82 +344,130 @@
         c.wait_send()
 
 
-def pair_up(panel, diag, level, parts):
-    n = lax.axis_size("space")
-    rows, modes = panel.shape
+def mixing_of(cross_gram, starts, level, snap_count):
+    snap = lax.axis_index("snap")
+    index = snap_count - (snap_count >> level) + snap // (1 << (level + 1))
+    return orthonormal(dot(cross_gram[...], starts[index], precision=HIGH)).astype(BF16)
+
+
+def pair_scratch(n, level, parts, rows_in, modes):
     half = parts // 2
-    rows_in = rows // parts
     members = 1 << (level + 1)
     share = modes // members
+    return [
+        pltpu.VMEM((half, rows_in, modes), BF16),
+        pltpu.VMEM((modes, modes), F32),
+        pltpu.VMEM((modes, modes), F32),
+        pltpu.VMEM((modes, modes), BF16),
+        pltpu.VMEM((members - 1, share, modes), BF16),
+        pltpu.VMEM((share, modes), BF16),
+        pltpu.VMEM((n - 1, share, modes), BF16),
+        pltpu.VMEM((share, modes), BF16),
+        pltpu.VMEM((members - 1, share, modes), BF16),
+        pltpu.SemaphoreType.DMA((2, half + 1)),
+        pltpu.SemaphoreType.DMA((2, members - 1)),
+        pltpu.SemaphoreType.DMA((2, n - 1)),
+        pltpu.SemaphoreType.DMA((2, members - 1)),
+        pltpu.VMEM((half, 2, rows_in, modes), BF16),
+        pltpu.VMEM((modes, modes), F32),
+        pltpu.VMEM((half * rows_in, 2 * modes), BF16),
+        pltpu.VMEM((2 * modes, 2 * modes), F32),
+    ]
+
+
+PER_LEVEL = 17
+
+
+def tree_kernel(n, snap_count, tri, start, weighted_in, starts, pair_out, gram_out, *scratch):
+    line, (gram, basis, weighted, sem) = scratch[:6], scratch[6:10]
+    snap = lax.axis_index("snap")
+    space = lax.axis_index("space")
+    load = pltpu.make_async_copy(weighted_in, weighted, sem)
+    load.start()
+    barrier = pltpu.get_barrier_semaphore()
+    for k in range(1, snap_count):
+        other = lax.rem(snap + k, snap_count)
+        pl.semaphore_signal(barrier, inc=1, device_id={"snap": other}, device_id_type=MESH)
+    for k in range(1, n):
+        other = lax.rem(space + k, n)
+        pl.semaphore_signal(barrier, inc=1, device_id={"space": other}, device_id_type=MESH)
+    pl.semaphore_wait(barrier, snap_count - 1 + n - 1)
+
+    line_sum(n, tri, *line)
+    levels = snap_count.bit_length() - 1
+    parts = snap_count
+    for level in range(levels):
+        own = scratch[10 + level * PER_LEVEL : 10 + (level + 1) * PER_LEVEL]
+        panel, diag, pair, cross_gram = own[13:]
+        rows = panel.shape[2]
+        if level == 0:
+            rounded = compress(line[0], start, gram, basis, diag)
+            load.wait()
+
+            def make(h, side):
+                low = pl.multiple_of((2 * h + side) * rows, rows)
+                return dot(weighted[pl.ds(low, rows), :], rounded).astype(BF16)
+        else:
+            mixing = mixing_of(below_gram, starts, level - 1, snap_count)
+            wide = mixing.astype(F32)
+            diag[...] = dot(wide, dot(below_gram[...], wide, precision=HIGH), TN, HIGH)
+
+            def make(h, side):
+                low = pl.multiple_of((2 * h + side) * rows, rows)
+                return dot(below[pl.ds(low, rows), :], mixing).astype(BF16)
+
+        if level == levels - 1:
+            pair, cross_gram = pair_out, gram_out
+        pair_up(n, level, make, diag, panel, pair, cross_gram, own[:13])
+        below, below_gram = pair, cross_gram
+
+
+def tree(tri, start_basis, weighted, merge_starts):
+    n = lax.axis_size("space")
+    snap_count = lax.axis_size("snap")
+    size, modes = start_basis.shape
+    rows_in = weighted.shape[0] // snap_count
+    scratch = [pltpu.VMEM(tri.shape, F32)]
+    scratch += [pltpu.VMEM(tri.shape, BF16)] * 4
+    scratch += [pltpu.SemaphoreType.DMA((4, tri.shape[0]))]
+    scratch += [
+        pltpu.VMEM((size, size), F32),
+        pltpu.VMEM((size, modes), F32),
+        pltpu.VMEM(weighted.shape, BF16),
+        pltpu.SemaphoreType.DMA,
+    ]
+    for level in range(snap_count.bit_length() - 1):
+        scratch += pair_scratch(n, level, snap_count >> level, rows_in, modes)
     return pl.pallas_call(
-        functools.partial(pair_kernel, n, level),
-        in_specs=[VMEM] * 2,
+        functools.partial(tree_kernel, n, snap_count),
+        in_specs=[VMEM, VMEM, pl.BlockSpec(memory_space=pl.ANY), VMEM],
         out_specs=[VMEM] * 2,
         out_shape=[
-            jax.ShapeDtypeStruct((rows // 2, 2 * modes), BF16),
+            jax.ShapeDtypeStruct((rows_in, 2 * modes), BF16),
             jax.ShapeDtypeStruct((2 * modes, 2 * modes), F32),
         ],
-        scratch_shapes=[
-            pltpu.VMEM((half, rows_in, modes), BF16),
-            pltpu.VMEM((modes, modes), F32),
-            pltpu.VMEM((modes, modes), F32),
-            pltpu.VMEM((modes, modes), BF16),
-            pltpu.VMEM((members - 1, share, modes), BF16),
-            pltpu.VMEM((share, modes), BF16),
-            pltpu.VMEM((n - 1, share, modes), BF16),
-            pltpu.VMEM((share, modes), BF16),
-            pltpu.VMEM((members - 1, share, modes), BF16),
-            pltpu.SemaphoreType.DMA((2, half + 1)),
-            pltpu.SemaphoreType.DMA((2, members - 1)),
-            pltpu.SemaphoreType.DMA((2, n - 1)),
-            pltpu.SemaphoreType.DMA((2, members - 1)),
-        ],
-        compiler_params=pltpu.CompilerParams(collective_id=1 + level, has_side_effects=True),
-        name="pair_up",
-    )(panel.reshape(half, 2, rows_in, modes), diag)
-
-
-def mix_kernel(snap_count, level, pair, cross_gram, starts, *outs):
-    snap = lax.axis_index("snap")
-    index = snap_count - (snap_count >> level) + snap // (1 << (level + 1))
-    steered = dot(cross_gram[...], starts[index], precision=HIGH)
-    mixing = orthonormal(steered).astype(BF16)
-    outs[0][...] = dot(pair[...], mixing).astype(BF16)
-    if len(outs) > 1:
-        wide = mixing.astype(F32)
-        outs[1][...] = dot(wide, dot(cross_gram[...], wide, precision=HIGH), TN, HIGH)
-
-
-def mix(pair, cross_gram, merge_starts, level, snap_count, last):
-    rows = pair.shape[0]
-    modes = merge_starts.shape[2]
-    shapes = [jax.ShapeDtypeStruct((rows, modes), BF16)]
-    if not last:
-        shapes.append(jax.ShapeDtypeStruct((modes, modes), F32))
+        scratch_shapes=scratch,
+        compiler_params=pltpu.CompilerParams(collective_id=0, has_side_effects=True),
+        name="tree",
+    )(tri, start_basis, weighted, merge_starts)
+
+
+def mix_kernel(snap_count, pair, cross_gram, starts, modes_ref):
+    level = snap_count.bit_length() - 2
+    mixing = mixing_of(cross_gram, starts, level, snap_count)
+    modes_ref[...] = dot(pair[...], mixing).astype(BF16)
+
+
+def local(snapshots, factor_blocks, factor_cols, factor_counts, start_basis, merge_starts):
+    weighted, tri = weigh(snapshots, factor_blocks, factor_cols, factor_counts)
+    pair, cross_gram = tree(tri, start_basis, weighted, merge_starts)
     return pl.pallas_call(
-        functools.partial(mix_kernel, snap_count, level),
+        functools.partial(mix_kernel, lax.axis_size("snap")),
         in_specs=[VMEM] * 3,
-        out_specs=[VMEM] * len(shapes),
-        out_shape=shapes,
+        out_specs=VMEM,
+        out_shape=jax.ShapeDtypeStruct((pair.shape[0], merge_starts.shape[2]), BF16),
         name="mix",
     )(pair, cross_gram, merge_starts)
-
-
-def local(snapshots, factor_blocks, factor_cols, factor_counts, start_basis, merge_starts):
-    weighted, tri = weigh(snapshots, factor_blocks, factor_cols, factor_counts)
-    tri = sum_over_space(tri)
-    panel, diag = compress(tri, start_basis, weighted)
-    parts = lax.axis_size("snap")
-    snap_count = parts
-    levels = snap_count.bit_length() - 1
-    for level in range(levels):
-        pair, cross_gram = pair_up(panel, diag, level, parts)
-        parts //= 2
-        last = level == levels - 1
-        made = mix(pair, cross_gram, merge_starts, level, snap_count, last)
-        panel = made[0]
-        diag = None if last else made[1]
-    return panel
 
 
 def solution(mesh):

time: 103 us -> 93.9 us (0.912)
  Pallas kernels: 103 us -> 93.6 us
    pallas_call x6 -> x2, Pallas kernels: 93.4 us -> 84.1 us  [the longest x1 76.3 us: tree(): pl.pallas_call(functools.partial(tree_kernel, n, snap_count), in_specs=[V...]
where the time goes in v3:
time: 93.9 us; the launch traced here: 93.6 us
  Pallas kernels  93.6 us (100%)
    pallas_call x1, Pallas kernels, tree(): pl.pallas_call(functools.partial(tree_kernel, n, snap_count), in_specs=[V...  76.3 us
    pallas_call x1, Pallas kernels, weigh(): pl.pallas_call(weigh_kernel, grid=(row_blocks // in_step,), in_specs=[pl....  9.57 us
    pallas_call x1, Pallas kernels, local(): pl.pallas_call(functools.partial(mix_kernel, lax.axis_size('snap')), in_s...  7.77 us

profile of v3, /device:TPU:0, one launch (start us, length us, event | category | flops | bytes accessed | tf_op | source)
XLA Modules:
  0.0 93.6 jit_solution(5638144194692589826)
XLA Ops:
  0.0 9.6 %weigh.1 = (bf16[4096,512]{1,0:T(8,128)(2,1)}, f32[10,128,128]{2,1,0:T(8,128)}) custom-call(s32[4,32]{1,0:T(4,128)} %bitcast.1, s32[32]{0:T(128)} %counts_ref.1, bf16[4096,512]{1,0:T(8,128)(2,1)} %snaps_ref.1, bf16[32,4,128,128]{3,2,1,0:T(8,128)(2,1)} %blocks_ref.1), custom_call_target="tpu_custom_call" | custom-call | tf_op jit(solution)/shard_map/weigh/pallas_call | solution.py:67
  9.6 76.3 %tree.1 = (bf16[1024,256]{1,0:T(8,128)(2,1)}, f32[256,256]{1,0:T(8,128)}) custom-call(f32[10,128,128]{2,1,0:T(8,128)} %get-tuple-element.9.tri, f32[512,128]{1,0:T(8,128)} %start.1, bf16[4096,512]{1,0:T(8,128)(2,1)} %get-tuple-element.10.weighted_in, f32[3,256,128]{2,1,0:T(8,128)} %starts.3), custom_call_target="tpu_custom_call" | custom-call | tf_op jit(solution)/shard_map/tree/pallas_call | solution.py:441
  85.9 7.8 %mix.1 = bf16[1024,128]{1,0:T(8,128)(2,1)} custom-call(bf16[1024,256]{1,0:T(8,128)(2,1)} %get-tuple-element.11.pair, f32[256,256]{1,0:T(8,128)} %get-tuple-element.12.cross_gram, f32[3,256,128]{2,1,0:T(8,128)} %starts.3), custom_call_target="tpu_custom_call" | custom-call | tf_op jit(solution)/shard_map/mix/pallas_call | solution.py:464

commit v4 on v3

--- a/solution.py
+++ b/solution.py
@@ -210,7 +210,7 @@
     return dot(z, inverse_factor(dot(z, z, TN, HIGH)), NT, HIGH)
 
 
-def compress(tri_ref, start_ref, gram, basis, diag_ref):
+def compress(tri_ref, start_ref, gram, basis):
     size = gram.shape[0]
     for index, (i, j) in enumerate(upper_blocks(size // 128)):
         block = tri_ref[index]
@@ -224,10 +224,12 @@
         return carry
 
     lax.fori_loop(0, 2, sweep, 0)
-    rounded = basis[...].astype(BF16)
-    wide = rounded.astype(F32)
-    diag_ref[...] = dot(wide, dot(gram[...], wide, precision=HIGH), TN, HIGH)
-    return rounded
+    return basis[...].astype(BF16)
+
+
+def projected(cross, vectors):
+    wide = vectors.astype(F32)
+    return dot(wide, dot(cross[...], wide, precision=HIGH), TN, HIGH)
 
 
 def flipped(index, bit):
@@ -245,7 +247,7 @@
     )
 
 
-def pair_up(n, level, make, diag, panel, pair, cross_gram, scratch):
+def pair_up(n, level, make, make_diag, diag, panel, pair, cross_gram, scratch):
     (got, got_diag, mine_all, out, came, z_out, z_came, sum_out, sum_came) = scratch[:9]
     sems, x_sems, z_sems, s_sems = scratch[9:]
     snap = lax.axis_index("snap")
@@ -271,9 +273,10 @@
     for h in range(half):
         panel[h, 1 - bit] = make(h, 1 - bit)
         copies[h].start()
-    copies[half].start()
     for h in range(half):
         panel[h, bit] = make(h, bit)
+    diag[...] = make_diag()
+    copies[half].start()
     cross = jnp.zeros((modes, modes), F32)
     upper = bit == 1
     for h in range(half):
@@ -401,24 +404,29 @@
         panel, diag, pair, cross_gram = own[13:]
         rows = panel.shape[2]
         if level == 0:
-            rounded = compress(line[0], start, gram, basis, diag)
+            rounded = compress(line[0], start, gram, basis)
             load.wait()
 
             def make(h, side):
                 low = pl.multiple_of((2 * h + side) * rows, rows)
                 return dot(weighted[pl.ds(low, rows), :], rounded).astype(BF16)
+
+            def make_diag():
+                return projected(gram, rounded)
+
         else:
             mixing = mixing_of(below_gram, starts, level - 1, snap_count)
-            wide = mixing.astype(F32)
-            diag[...] = dot(wide, dot(below_gram[...], wide, precision=HIGH), TN, HIGH)
 
             def make(h, side):
                 low = pl.multiple_of((2 * h + side) * rows, rows)
                 return dot(below[pl.ds(low, rows), :], mixing).astype(BF16)
 
+            def make_diag():
+                return projected(below_gram, mixing)
+
         if level == levels - 1:
             pair, cross_gram = pair_out, gram_out
-        pair_up(n, level, make, diag, panel, pair, cross_gram, own[:13])
+        pair_up(n, level, make, make_diag, diag, panel, pair, cross_gram, own[:13])
         below, below_gram = pair, cross_gram
 
 

time: 93.9 us -> 92 us (0.980)
  Pallas kernels: 93.6 us -> 91.8 us
    pallas_call x1, Pallas kernels: 76.3 us -> 74.5 us  [tree(): pl.pallas_call(functools.partial(tree_kernel, n, snap_count), in_specs=[V...]
where the time goes in v4:
time: 92 us; the launch traced here: 91.8 us
  Pallas kernels  91.8 us (100%)
    pallas_call x1, Pallas kernels, tree(): pl.pallas_call(functools.partial(tree_kernel, n, snap_count), in_specs=[V...  74.5 us
    pallas_call x1, Pallas kernels, weigh(): pl.pallas_call(weigh_kernel, grid=(row_blocks // in_step,), in_specs=[pl....  9.57 us
    pallas_call x1, Pallas kernels, local(): pl.pallas_call(functools.partial(mix_kernel, lax.axis_size('snap')), in_s...  7.77 us

profile of v4, /device:TPU:0, one launch (start us, length us, event | category | flops | bytes accessed | tf_op | source)
XLA Modules:
  0.0 91.8 jit_solution(3460828019861578151)
XLA Ops:
  0.0 9.6 %weigh.1 = (bf16[4096,512]{1,0:T(8,128)(2,1)}, f32[10,128,128]{2,1,0:T(8,128)}) custom-call(s32[4,32]{1,0:T(4,128)} %bitcast.1, s32[32]{0:T(128)} %counts_ref.1, bf16[4096,512]{1,0:T(8,128)(2,1)} %snaps_ref.1, bf16[32,4,128,128]{3,2,1,0:T(8,128)(2,1)} %blocks_ref.1), custom_call_target="tpu_custom_call" | custom-call | tf_op jit(solution)/shard_map/weigh/pallas_call | solution.py:67
  9.6 74.5 %tree.1 = (bf16[1024,256]{1,0:T(8,128)(2,1)}, f32[256,256]{1,0:T(8,128)}) custom-call(f32[10,128,128]{2,1,0:T(8,128)} %get-tuple-element.9.tri, f32[512,128]{1,0:T(8,128)} %start.1, bf16[4096,512]{1,0:T(8,128)(2,1)} %get-tuple-element.10.weighted_in, f32[3,256,128]{2,1,0:T(8,128)} %starts.3), custom_call_target="tpu_custom_call" | custom-call | tf_op jit(solution)/shard_map/tree/pallas_call | solution.py:449
  84.0 7.8 %mix.1 = bf16[1024,128]{1,0:T(8,128)(2,1)} custom-call(bf16[1024,256]{1,0:T(8,128)(2,1)} %get-tuple-element.11.pair, f32[256,256]{1,0:T(8,128)} %get-tuple-element.12.cross_gram, f32[3,256,128]{2,1,0:T(8,128)} %starts.3), custom_call_target="tpu_custom_call" | custom-call | tf_op jit(solution)/shard_map/mix/pallas_call | solution.py:472
